TPU v7x, 32 devices: a whole 2x2x4 slice. The times are simulated.
32 devices in a mesh: seq: 8 (over z, y), head: 4 (over x, core).
Axes of the slice: x: 2, y: 2, z: 4, core: 2. Of those that a mesh axis runs over, the one named last changes fastest.
Arguments:
- queries: bfloat16 [2, 64, 64, 128], P(None, 'head'), may hold values from -9 to 9
- cache_keys: bfloat16 [2, 8, 8192, 128], P(None, 'head', 'seq'), may hold values from -10 to 10
- cache_values: bfloat16 [2, 8, 8192, 128], P(None, 'head', 'seq'), may hold values from -6 to 6
- new_keys: bfloat16 [2, 8, 64, 128], P(None, 'head'), may hold values from -20 to 20
- new_values: bfloat16 [2, 8, 64, 128], P(None, 'head'), may hold values from -6 to 6
- parents: int32 [2, 64], replicated, may hold values from 0 to 62, as said below
- path: int32 [2, 6], replicated, may hold values from 0 to 63, as said below
- lengths: int32 [2], replicated, may hold values from 2048 to 8192, as said below
- draft_tokens: int32 [2, 64], replicated, may hold values from 0 to 65535
- residual: bfloat16 [2, 64, 8192], P(None, None, 'seq'), may hold values from -8 to 8
- out_weight: bfloat16 [8192, 8192], P('head', 'seq'), may hold values from -0.0625 to 0.0625
- norm_gain: bfloat16 [8192], P('seq'), may hold values from 0.5 to 1.5
- vocab_weight: bfloat16 [8192, 65536], P(None, ('seq', 'head')), may hold values from -3 to 3
Outputs:
- path_logits: float32 [2, 6, 65536], P(None, None, ('seq', 'head'))
- draft_logprob: float32 [2, 64], replicated
Inputs may be any that keep to these rules, and one draw needn't show every extreme that they name: parents[b, 0] is 0; for every other node n, parents[b, n] is a smaller node number. path[b] lists 6 different nodes: node 0 first, and each later entry is a child (by parents) of the entry before it. `lengths`: at least one sequence uses all 8192 cache positions.
All inputs are finite; a program needn't handle non-finite values.
Results may differ from a plain program's by a relative error of at most 0.006.
Values may be sent and summed in bfloat16 or wider, within the bound.
A program may use at most 128 MiB of HBM per device.

v0:
```python
import jax
import jax.numpy as jnp
from jax import lax
from jax.sharding import PartitionSpec as P

D = 8192
lowest = -1e30
epsilon = 1e-05


def ancestors(parents):
    node_count = parents.shape[-1]
    node_ids = jnp.arange(node_count, dtype=jnp.int32)
    linked = (parents[..., :, None] == node_ids[None, None, :]).astype(jnp.float32)
    reached = jnp.maximum(linked, jnp.eye(node_count, dtype=jnp.float32)[None])
    for _ in range(node_count.bit_length()):
        reached = jnp.minimum(jnp.einsum("bij,bjk->bik", reached, reached), 1.0)
    return reached > 0.5


def block_state(scores, visible, values):
    masked = jnp.where(visible, scores, lowest)
    block_max = jnp.max(masked, axis=-1)
    weights = jnp.where(visible, jnp.exp(masked - block_max[..., None]), 0.0).astype(jnp.bfloat16)
    block_total = jnp.sum(weights.astype(jnp.float32), axis=-1)
    block_out = jnp.einsum("kqc,kcd->kqd", weights, values, preferred_element_type=jnp.float32)
    return (block_max, block_total, block_out)


def join_states(earlier, later):
    summit = jnp.maximum(earlier[0], later[0])
    damp_early = jnp.exp(earlier[0] - summit)
    damp_later = jnp.exp(later[0] - summit)
    total_joined = earlier[1] * damp_early + later[1] * damp_later
    out_joined = earlier[2] * damp_early[..., None] + later[2] * damp_later[..., None]
    return (summit, total_joined, out_joined)


def on_device(
    queries,
    cache_keys,
    cache_values,
    new_keys,
    new_values,
    parents,
    path,
    lengths,
    draft_tokens,
    residual,
    out_weight,
    norm_gain,
    vocab_weight,
):
    batch_size, heads_local, node_count, head_dim = queries.shape
    kv_local = cache_keys.shape[1]
    span_local = cache_keys.shape[2]
    group_size = heads_local // kv_local
    score_scale = head_dim ** (-0.5)
    seq_index = lax.axis_index("seq")
    reached = ancestors(parents)
    is_owner = seq_index == 0
    offsets = seq_index * span_local + jnp.arange(span_local, dtype=jnp.int32)

    def per_sequence(entries):
        query_block, key_block, value_block, tree_keys, tree_values, reach_row, length = entries
        grouped = query_block.reshape(kv_local, group_size * node_count, head_dim)
        scores = (
            jnp.einsum("kqd,kcd->kqc", grouped, key_block, preferred_element_type=jnp.float32)
            * score_scale
        )
        live_keys = (offsets < length)[None, None, :]
        cache_state = block_state(scores, live_keys, value_block)
        tree_scores = (
            jnp.einsum("kqd,kcd->kqc", grouped, tree_keys, preferred_element_type=jnp.float32)
            * score_scale
        )
        tree_seen = jnp.logical_and(jnp.tile(reach_row, (group_size, 1))[None], is_owner)
        tree_state = block_state(tree_scores, tree_seen, tree_values)
        return join_states(cache_state, tree_state)

    maxima, totals, outputs = lax.map(
        per_sequence, (queries, cache_keys, cache_values, new_keys, new_values, reached, lengths)
    )
    weight_heads = out_weight.reshape(heads_local, head_dim, -1)
    highest = lax.pmax(maxima, "seq")
    factors = jnp.exp(maxima - highest)
    scaled = (outputs * factors[..., None]).reshape(batch_size, heads_local, node_count, head_dim)
    summed = (totals * factors).reshape(batch_size, heads_local, node_count)
    share_out, share_total = (
        lax.psum_scatter(scaled, "seq", scatter_dimension=2, tiled=True),
        lax.psum_scatter(summed, "seq", scatter_dimension=2, tiled=True),
    )
    attention = (share_out / share_total[..., None]).astype(jnp.bfloat16)
    projected = jnp.einsum(
        "bhnd,hdc->bnc",
        lax.all_gather(attention, "seq", axis=2, tiled=True),
        weight_heads,
        preferred_element_type=jnp.float32,
    )
    vocab_local = vocab_weight.shape[1]
    projected = lax.psum(projected, "head")
    stream = residual.astype(jnp.float32) + projected
    gain_part = norm_gain.astype(jnp.float32)
    square_sum = lax.psum(jnp.sum(stream * stream, axis=-1), "seq")
    normed = (stream * lax.rsqrt(square_sum / D + epsilon)[..., None] * gain_part).astype(
        jnp.bfloat16
    )
    portion = lax.all_gather(normed, "seq", axis=2, tiled=True)
    flat_part = portion.reshape(batch_size * node_count, portion.shape[2])
    logits = jnp.dot(flat_part, vocab_weight, preferred_element_type=jnp.float32)
    logits = logits.reshape(batch_size, node_count, vocab_local)
    vocab_first = lax.axis_index(("seq", "head")) * vocab_local
    vocab_ids = jnp.arange(vocab_local, dtype=jnp.int32) + vocab_first
    picked = jnp.sum(jnp.where(draft_tokens[..., None] == vocab_ids, logits, 0.0), axis=-1)
    local_max = jnp.max(logits, axis=-1)
    vocab_top = lax.pmax(local_max, ("seq", "head"))
    local_sum = jnp.sum(jnp.exp(logits - vocab_top[..., None]), axis=-1)
    exp_sums, picked = lax.psum((local_sum, picked), ("seq", "head"))
    draft_logprob = picked - (vocab_top + jnp.log(exp_sums))
    path_logits = jnp.take_along_axis(logits, path[:, :, None], axis=1)
    return (path_logits, draft_logprob)


def solution(mesh):
    placed = (
        P(None, "head", None, None),
        P(None, "head", "seq", None),
        P(None, "head", "seq", None),
        P(None, "head", None, None),
        P(None, "head", None, None),
        P(),
        P(),
        P(),
        P(),
        P(None, None, "seq"),
        P("head", "seq"),
        P("seq"),
        P(None, ("seq", "head")),
    )
    return jax.shard_map(
        on_device,
        mesh=mesh,
        in_specs=placed,
        out_specs=(P(None, None, ("seq", "head")), P()),
        check_vma=False,
    )
```

profile of v0, /device:TPU:0, one launch (start us, length us, event | category | flops | bytes accessed | tf_op | source)
XLA Modules:
  0.0 349.0 jit_solution(16134530394701500435)
XLA Ops:
  9.1 17.6 %while.15 = (s32[]{:T(128)}, f32[2,2,512]{2,1,0:T(2,128)S(1)}, f32[2,2,512]{2,1,0:T(2,128)S(1)}, f32[2,2,512,128]{3,2,1,0:T(8,128)S(1)}, s32[2]{0:T(128)}, /*ind...) while((s32[]{:T(128)}, f32[2,2,512]{2,1,0:T(2,128)S(1)}, ...), condition=%wide.region_5.6_spmd.clone, body=%wide.region_0.5_spmd.clone.sunk | while | flops 587279360 | bytes 21873904 | solution.py:81
  11.5 1.2 dynamic_slice.68
  13.3 2.0 fusion.70
  15.3 1.2 convert_reduce_fusion.5
  16.9 1.1 fusion.73
  20.3 1.2 dynamic_slice.68
  22.1 2.0 fusion.70
  24.1 1.2 convert_reduce_fusion.5
  25.7 1.1 fusion.73
  26.7 23.4 %pmax.14 = f32[2,2,512]{2,1,0:T(2,128)S(1)} all-reduce(f32[2,2,512]{2,1,0:T(2,128)S(1)} %get-tuple-element.72), channel_id=1, replica_groups=mesh['seq'=8,'head'=4] {'seq'}, use_global_device_ids=true, to_apply=%region_6.7 | all-reduce | flops 2048 | bytes 16384 | tf_op jit(solution)/shard_map/pmax | solution.py:85
  50.2 1.3 broadcast_multiply_fusion
  53.0 33.4 %all-reduce = f32[2,16,64]{1,0,2:T(2,128)S(1)} all-reduce(f32[2,16,64]{1,0,2:T(2,128)S(1)} %copy.24), channel_id=3, replica_groups=mesh['seq'=8,'head'=4] {'seq'}, use_global_device_ids=true, to_apply=%region_8.9.clone | all-reduce | flops 2048 | bytes 16384
  86.6 27.2 %reduce-scatter.2.cloned.1.call-done = f32[2,16,8,128]{3,2,1,0:T(8,128)} async-done(((f32[2,16,64,128]{3,2,1,0:T(8,128)}), f32[2,16,8,128]{3,2,1,0:T(8,128)}) %reduce-scatter.2.cloned.1.call-update) | async-done | bytes 131088 | tf_op jit(solution)/shard_map/reduce_scatter | solution.py:90
  113.7 1.0 divide_convert_fusion
  114.7 27.1 %all_gather.6 = bf16[2,16,64,128]{3,2,1,0:T(8,128)(2,1)S(1)} all-gather(bf16[2,16,8,128]{3,2,1,0:T(8,128)(2,1)S(1)} %divide_convert_fusion), channel_id=1, replica_groups=mesh['seq'=8,'head'=4] {'seq'}, dimensions={2}, use_global_device_ids=true | all-gather | bytes 589824 | tf_op jit(solution)/shard_map/all_gather | solution.py:96
  141.9 3.8 %convolution_bitcast_fusion = f32[2,64,1024]{2,1,0:T(8,128)} fusion(bf16[2,16,64,128]{3,2,1,0:T(8,128)(2,1)S(1)} %all_gather.6, bf16[16,128,1024,1]{2,1,0,3:T(8,128)(2,1)} %bitcast.116), kind=kOutput, calls=%fused_computation.49 | convolution fusion | flops 536870912 | bytes 5242880 | tf_op jit(solution)/shard_map/bhnd,hdc->bnc/dot_general | solution.py:94
  145.8 31.3 %all-reduce.4.cloned.1.call-done = f32[2,64,1024]{2,1,0:T(8,128)} async-done(((f32[2,64,1024]{2,1,0:T(8,128)}), f32[2,64,1024]{2,1,0:T(8,128)}) %all-reduce.4.cloned.1.call-update) | async-done | bytes 524304 | tf_op jit(solution)/shard_map/psum | solution.py:101
  177.1 1.2 multiply_reduce_fusion
  178.3 21.4 %psum.29 = f32[2,64]{1,0:T(2,128)S(1)} all-reduce(f32[2,64]{1,0:T(2,128)S(1)} %multiply_reduce_fusion), channel_id=1, replica_groups=mesh['seq'=8,'head'=4] {'seq'}, use_global_device_ids=true, to_apply=%region_11.12 | all-reduce | flops 128 | bytes 1024 | tf_op jit(solution)/shard_map/psum | solution.py:104
  199.7 1.9 multiply_convert_fusion
  201.7 45.5 %all-gather.2.cloned.1.call-done = bf16[2,64,8192]{2,1,0:T(8,128)(2,1)} async-done(((bf16[2,64,1024]{2,1,0:T(8,128)(2,1)}), bf16[2,64,8192]{2,1,0:T(8,128)(2,1)}) %all-gather.2.cloned.1.call-update) | async-done | bytes 2097168 | tf_op jit(solution)/shard_map/all_gather | solution.py:108
  247.2 13.6 %fusion.44 = (f32[2,64]{1,0:T(2,128)S(1)}, f32[2,64,2048]{2,1,0:T(8,128)S(1)}) fusion(bf16[2,64,8192]{2,1,0:T(8,128)(2,1)} %all-gather.2.cloned.1.call-done, bf16[8192,2048]{1,0:T(8,128)(2,1)} %param.27), kind=kOutput, calls=%fused_computation.89 | convolution fusion | flops 4295229440 | bytes 36700672 | tf_op jit(solution)/shard_map/dot_general | solution.py:110
  262.4 39.2 %pmax.15 = f32[2,64]{1,0:T(2,128)S(1)} all-reduce(f32[2,64]{1,0:T(2,128)S(1)} %get-tuple-element.201), channel_id=1, replica_groups=mesh['seq'=8,'head'=4] {'seq','head'}, use_global_device_ids=true, to_apply=%region_15.16 | all-reduce | flops 128 | bytes 1024 | tf_op jit(solution)/shard_map/pmax | solution.py:116
  301.9 40.0 %all-reduce.1 = (f32[2,64]{1,0:T(2,128)S(1)}, f32[2,64]{1,0:T(2,128)S(1)}) all-reduce(f32[2,64]{1,0:T(2,128)S(1)} %get-tuple-element.162, f32[2,64]{1,0:T(2,128)S(1)} %get-tuple-element.161), channel_id=1, replica_groups=mesh['seq'=8,'head'=4] {'seq','head'}, use_global_device_ids=true, to_apply=%region_13.14 | all-reduce | flops 256 | bytes 2048 | tf_op jit(solution)/shard_map/psum | solution.py:118
  (74 shorter events, 12.1 us)
Async XLA Ops:
  7.2 106.6 %reduce-scatter.2.cloned.1.call-start = ((), (), s32[]{:S(2)}) async-start(), calls=%async_computation.1 | async-start | bytes 1179648 | tf_op jit(solution)/shard_map/reduce_scatter | solution.py:90
  9.1 42.7 %copy-start.6 = (u32[32]{0:T(128)S(1)}, u32[32]{0:T(128)}, u32[]{:S(2)}) copy-start(u32[32]{0:T(128)} %constant.93) | copy-start | bytes 388
  13.3 3.2 copy-start.1
  13.3 3.5 %copy-start.5 = (bf16[2,2,1024,128]{3,2,1,0:T(8,128)(2,1)S(1)}, bf16[2,2,1024,128]{3,2,1,0:T(8,128)(2,1)}, u32[]{:S(2)}) copy-start(bf16[2,2,1024,128]{3,2,1,0:T(8,128)(2,1)} %get-tuple-element.336) | copy-start | bytes 3145732 | tf_op jit(solution)/shard_map/while
  22.1 3.2 copy-start.1
  22.1 3.5 %copy-start.5 = (bf16[2,2,1024,128]{3,2,1,0:T(8,128)(2,1)S(1)}, bf16[2,2,1024,128]{3,2,1,0:T(8,128)(2,1)}, u32[]{:S(2)}) copy-start(bf16[2,2,1024,128]{3,2,1,0:T(8,128)(2,1)} %get-tuple-element.336) | copy-start | bytes 3145732 | tf_op jit(solution)/shard_map/while
  51.5 125.6 %all-reduce.4.cloned.1.call-start = ((), (), s32[]{:S(2)}) async-start(), calls=%async_computation.2 | async-start | bytes 1048576 | tf_op jit(solution)/shard_map/psum | solution.py:101
  86.4 59.3 %copy-start.2 = (bf16[1024]{0:T(1024)(128)(2,1)S(1)}, bf16[1024]{0:T(1024)(128)(2,1)}, u32[]{:S(2)}) copy-start(bf16[1024]{0:T(1024)(128)(2,1)} %param.26) | copy-start | bytes 6148
  86.4 90.7 %copy-start = (bf16[2,64,1024]{2,1,0:T(8,128)(2,1)S(1)}, bf16[2,64,1024]{2,1,0:T(8,128)(2,1)}, u32[]{:S(2)}) copy-start(bf16[2,64,1024]{2,1,0:T(8,128)(2,1)} %param.24) | copy-start | bytes 786436
  141.9 59.7 %copy-start.3 = (s32[2,6]{1,0:T(2,128)S(1)}, s32[2,6]{1,0:T(2,128)}, u32[]{:S(2)}) copy-start(s32[2,6]{1,0:T(2,128)} %param.21) | copy-start | bytes 148
  145.7 101.5 %all-gather.2.cloned.1.call-start = ((), (), s32[]{:S(2)}) async-start(), calls=%async_computation.3 | async-start | bytes 2359296 | tf_op jit(solution)/shard_map/all_gather | solution.py:108
  201.7 99.9 %copy-start.4 = (s32[2,64]{1,0:T(2,128)S(1)}, s32[2,64]{1,0:T(2,128)}, u32[]{:S(2)}) copy-start(s32[2,64]{1,0:T(2,128)} %param.23) | copy-start | bytes 1540
Sparse Core Ops, SparseCore 0:
  51.6 62.0 reduce-scatter.1
  145.8 31.2 all-reduce.3
  201.7 45.4 all-gather.1
where the time goes:
time: 350 us; the launch traced here: 349 us
  blocking collectives  184 us (53%)
  waiting for transfers between devices  104 us (30%)
  matrix products  27.8 us (8%)
  between operations  14.6 us (4%)
  other arithmetic  10.2 us (3%)
  local copies, waits for them, and re-layouts  7.47 us (2%)
    all_gather x1, waiting for transfers between devices, on_device(): portion = lax.all_gather(normed, 'seq', axis=2, tiled=True)  45.5 us
    psum x1, blocking collectives, on_device(): exp_sums, picked = lax.psum((local_sum, picked), ('seq', 'head'))  40 us
    pmax x1, blocking collectives, on_device(): vocab_top = lax.pmax(local_max, ('seq', 'head'))  39.2 us
    unnamed x1, blocking collectives  33.4 us
    psum x1, waiting for transfers between devices, on_device(): projected = lax.psum(projected, 'head')  31.3 us
    reduce_scatter x1, waiting for transfers between devices, on_device(): lax.psum_scatter(scaled, 'seq', scatter_dimension=2, tiled=True)  27.2 us
    all_gather x1, blocking collectives, on_device(): lax.all_gather(attention, 'seq', axis=2, tiled=True)  27.1 us
    pmax x1, blocking collectives, on_device(): highest = lax.pmax(maxima, 'seq')  23.4 us
  transfers between devices with their start and end apart: 3, of which 3 were waited for; matrix products, arithmetic and copies ran while one was open for 0% of the time, Pallas kernels for 0%

commit v1 on v0

--- a/solution.py
+++ b/solution.py
@@ -6,6 +6,17 @@
 D = 8192
 lowest = -1e30
 epsilon = 1e-05
+
+
+def seats_all_produce(vec):
+    before = vec
+    dev_n = lax.psum(1, "head")
+    for k in [
+        [(w, w ^ dev_j) for w in range(dev_n)] for dev_j in (1, 2, 4, 8, 16) if dev_j < dev_n
+    ]:
+        passed = lax.ppermute(before, "head", k)
+        before = before + passed
+    return before
 
 
 def ancestors(parents):
@@ -98,7 +109,7 @@
         preferred_element_type=jnp.float32,
     )
     vocab_local = vocab_weight.shape[1]
-    projected = lax.psum(projected, "head")
+    projected = seats_all_produce(projected)
     stream = residual.astype(jnp.float32) + projected
     gain_part = norm_gain.astype(jnp.float32)
     square_sum = lax.psum(jnp.sum(stream * stream, axis=-1), "seq")

time: 350 us -> 330 us (0.943)
  waiting for transfers between devices: 104 us -> 88.2 us
    psum x1 -> x0, waiting for transfers between devices: 31.3 us -> none  [on_device(): projected = lax.psum(projected, 'head')]
    ppermute x0 -> x2, waiting for transfers between devices: none -> 14.3 us  [seats_all_produce(): passed = lax.ppermute(before, 'head', k)]
  transfers between devices with their start and end apart: 3 -> 4, of which waited for: 3 -> 4; matrix products, arithmetic and copies ran while one was open for 0% -> 0% of each run, Pallas kernels for 0% -> 0%
where the time goes in v1:
time: 330 us; the launch traced here: 329 us
  blocking collectives  181 us (55%)
  waiting for transfers between devices  88.2 us (27%)
  matrix products  27 us (8%)
  between operations  14.9 us (5%)
  other arithmetic  8.25 us (2%)
  local copies, waits for them, and re-layouts  7.46 us (2%)
    all_gather x1, waiting for transfers between devices, on_device(): portion = lax.all_gather(normed, 'seq', axis=2, tiled=True)  46.7 us
    psum x1, blocking collectives, on_device(): exp_sums, picked = lax.psum((local_sum, picked), ('seq', 'head'))  40 us
    pmax x1, blocking collectives, on_device(): vocab_top = lax.pmax(local_max, ('seq', 'head'))  39.2 us
    unnamed x1, blocking collectives  33.4 us
    reduce_scatter x1, waiting for transfers between devices, on_device(): lax.psum_scatter(scaled, 'seq', scatter_dimension=2, tiled=True)  27.2 us
    all_gather x1, blocking collectives, on_device(): lax.all_gather(attention, 'seq', axis=2, tiled=True)  27.2 us
    pmax x1, blocking collectives, on_device(): highest = lax.pmax(maxima, 'seq')  23.4 us
    psum x1, blocking collectives, on_device(): square_sum = lax.psum(jnp.sum(stream * stream, axis=-1), 'seq')  18.3 us
  transfers between devices with their start and end apart: 4, of which 4 were waited for; matrix products, arithmetic and copies ran while one was open for 0% of the time, Pallas kernels for 0%

profile of v1, /device:TPU:0, one launch (start us, length us, event | category | flops | bytes accessed | tf_op | source)
XLA Modules:
  0.0 329.1 jit_solution(9262301445488805071)
XLA Ops:
  9.1 17.6 %while.15 = (s32[]{:T(128)}, f32[2,2,512]{2,1,0:T(2,128)S(1)}, f32[2,2,512]{2,1,0:T(2,128)S(1)}, f32[2,2,512,128]{3,2,1,0:T(8,128)S(1)}, s32[2]{0:T(128)}, /*ind...) while((s32[]{:T(128)}, f32[2,2,512]{2,1,0:T(2,128)S(1)}, ...), condition=%wide.region_5.6_spmd.clone, body=%wide.region_0.5_spmd.clone.sunk | while | flops 587279360 | bytes 21873904 | solution.py:92
  11.5 1.2 dynamic_slice.68
  13.3 2.0 fusion.70
  15.3 1.2 convert_reduce_fusion.5
  16.9 1.0 fusion.73
  20.3 1.2 dynamic_slice.68
  22.1 2.0 fusion.70
  24.1 1.2 convert_reduce_fusion.5
  25.7 1.0 fusion.73
  26.7 23.4 %pmax.14 = f32[2,2,512]{2,1,0:T(2,128)S(1)} all-reduce(f32[2,2,512]{2,1,0:T(2,128)S(1)} %get-tuple-element.72), channel_id=1, replica_groups=mesh['seq'=8,'head'=4] {'seq'}, use_global_device_ids=true, to_apply=%region_6.7 | all-reduce | flops 2048 | bytes 16384 | tf_op jit(solution)/shard_map/pmax | solution.py:96
  50.2 1.3 broadcast_multiply_fusion
  53.0 33.4 %all-reduce = f32[2,16,64]{1,0,2:T(2,128)S(1)} all-reduce(f32[2,16,64]{1,0,2:T(2,128)S(1)} %copy.24), channel_id=3, replica_groups=mesh['seq'=8,'head'=4] {'seq'}, use_global_device_ids=true, to_apply=%region_8.9.clone | all-reduce | flops 2048 | bytes 16384
  86.5 27.2 %reduce-scatter.2.cloned.1.call-done = f32[2,16,8,128]{3,2,1,0:T(8,128)} async-done(((f32[2,16,64,128]{3,2,1,0:T(8,128)}), f32[2,16,8,128]{3,2,1,0:T(8,128)}) %reduce-scatter.2.cloned.1.call-update) | async-done | bytes 131088 | tf_op jit(solution)/shard_map/reduce_scatter | solution.py:101
  113.7 1.0 divide_convert_fusion
  114.7 27.2 %all_gather.6 = bf16[2,16,64,128]{3,2,1,0:T(8,128)(2,1)S(1)} all-gather(bf16[2,16,8,128]{3,2,1,0:T(8,128)(2,1)S(1)} %divide_convert_fusion), channel_id=1, replica_groups=mesh['seq'=8,'head'=4] {'seq'}, dimensions={2}, use_global_device_ids=true | all-gather | bytes 589824 | tf_op jit(solution)/shard_map/all_gather | solution.py:107
  141.9 2.9 convolution_bitcast_fusion
  144.9 1.9 collective-permute-done
  146.9 1.6 collective-permute-start.1
  148.5 12.4 %collective-permute-done.1 = f32[2,64,1024]{2,1,0:T(8,128)S(1)} collective-permute-done((f32[2,64,1024]{2,1,0:T(8,128)S(1)}, f32[2,64,1024]{2,1,0:T(8,128)S(1)}, u32[]{:S(2)}, u32[]{:S(2)}) %collective-permute-start.1) | collective-permute-done | bytes 524320 | tf_op jit(solution)/shard_map/ppermute | solution.py:17
  161.1 18.3 %psum.21 = f32[2,64]{1,0:T(2,128)S(1)} all-reduce(f32[2,64]{1,0:T(2,128)S(1)} %multiply_reduce_fusion), channel_id=1, replica_groups=mesh['seq'=8,'head'=4] {'seq'}, use_global_device_ids=true, to_apply=%region_10.11 | all-reduce | flops 128 | bytes 1024 | tf_op jit(solution)/shard_map/psum | solution.py:115
  180.4 46.7 %all-gather.2.cloned.1.call-done = bf16[2,64,8192]{2,1,0:T(8,128)(2,1)} async-done(((bf16[2,64,1024]{2,1,0:T(8,128)(2,1)}), bf16[2,64,8192]{2,1,0:T(8,128)(2,1)}) %all-gather.2.cloned.1.call-update) | async-done | bytes 2097168 | tf_op jit(solution)/shard_map/all_gather | solution.py:119
  227.1 13.6 %fusion.44 = (f32[2,64]{1,0:T(2,128)S(1)}, f32[2,64,2048]{2,1,0:T(8,128)S(1)}) fusion(bf16[2,64,8192]{2,1,0:T(8,128)(2,1)} %all-gather.2.cloned.1.call-done, bf16[8192,2048]{1,0:T(8,128)(2,1)} %param.27), kind=kOutput, calls=%fused_computation.89 | convolution fusion | flops 4295229440 | bytes 36700672 | tf_op jit(solution)/shard_map/dot_general | solution.py:121
  242.2 39.2 %pmax.15 = f32[2,64]{1,0:T(2,128)S(1)} all-reduce(f32[2,64]{1,0:T(2,128)S(1)} %get-tuple-element.201), channel_id=1, replica_groups=mesh['seq'=8,'head'=4] {'seq','head'}, use_global_device_ids=true, to_apply=%region_14.15 | all-reduce | flops 128 | bytes 1024 | tf_op jit(solution)/shard_map/pmax | solution.py:127
  281.8 40.0 %all-reduce.1 = (f32[2,64]{1,0:T(2,128)S(1)}, f32[2,64]{1,0:T(2,128)S(1)}) all-reduce(f32[2,64]{1,0:T(2,128)S(1)} %get-tuple-element.162, f32[2,64]{1,0:T(2,128)S(1)} %get-tuple-element.161), channel_id=1, replica_groups=mesh['seq'=8,'head'=4] {'seq','head'}, use_global_device_ids=true, to_apply=%region_12.13 | all-reduce | flops 256 | bytes 2048 | tf_op jit(solution)/shard_map/psum | solution.py:129
  (76 shorter events, 13.2 us)
Async XLA Ops:
  7.2 106.6 %reduce-scatter.2.cloned.1.call-start = ((), (), s32[]{:S(2)}) async-start(), calls=%async_computation.1 | async-start | bytes 1179648 | tf_op jit(solution)/shard_map/reduce_scatter | solution.py:101
  9.1 42.7 %copy-start.6 = (u32[32]{0:T(128)S(1)}, u32[32]{0:T(128)}, u32[]{:S(2)}) copy-start(u32[32]{0:T(128)} %constant.93) | copy-start | bytes 388
  13.3 3.2 copy-start.1
  13.3 3.5 %copy-start.5 = (bf16[2,2,1024,128]{3,2,1,0:T(8,128)(2,1)S(1)}, bf16[2,2,1024,128]{3,2,1,0:T(8,128)(2,1)}, u32[]{:S(2)}) copy-start(bf16[2,2,1024,128]{3,2,1,0:T(8,128)(2,1)} %get-tuple-element.336) | copy-start | bytes 3145732 | tf_op jit(solution)/shard_map/while
  22.1 3.2 copy-start.1
  22.1 3.5 %copy-start.5 = (bf16[2,2,1024,128]{3,2,1,0:T(8,128)(2,1)S(1)}, bf16[2,2,1024,128]{3,2,1,0:T(8,128)(2,1)}, u32[]{:S(2)}) copy-start(bf16[2,2,1024,128]{3,2,1,0:T(8,128)(2,1)} %get-tuple-element.336) | copy-start | bytes 3145732 | tf_op jit(solution)/shard_map/while
  51.5 175.5 %all-gather.2.cloned.1.call-start = ((), (), s32[]{:S(2)}) async-start(), calls=%async_computation.2 | async-start | bytes 2359296 | tf_op jit(solution)/shard_map/all_gather | solution.py:119
  141.9 6.6 %copy-start.2 = (bf16[1024]{0:T(1024)(128)(2,1)S(1)}, bf16[1024]{0:T(1024)(128)(2,1)}, u32[]{:S(2)}) copy-start(bf16[1024]{0:T(1024)(128)(2,1)} %param.26) | copy-start | bytes 6148
  141.9 19.0 %copy-start = (bf16[2,64,1024]{2,1,0:T(8,128)(2,1)S(1)}, bf16[2,64,1024]{2,1,0:T(8,128)(2,1)}, u32[]{:S(2)}) copy-start(bf16[2,64,1024]{2,1,0:T(8,128)(2,1)} %param.24) | copy-start | bytes 786436
  141.9 38.4 %copy-start.3 = (s32[2,6]{1,0:T(2,128)S(1)}, s32[2,6]{1,0:T(2,128)}, u32[]{:S(2)}) copy-start(s32[2,6]{1,0:T(2,128)} %param.21) | copy-start | bytes 148
  144.9 2.0 collective-permute-start
  146.9 14.0 %collective-permute-start.1 = (f32[2,64,1024]{2,1,0:T(8,128)S(1)}, f32[2,64,1024]{2,1,0:T(8,128)S(1)}, u32[]{:S(2)}, u32[]{:S(2)}) collective-permute-start(f32[2,64,1024]{2,1,0:T(8,128)S(1)} %add.71), channel_id=1, source_target_pairs={{0,2},{1,3},{2,0},{3,1},{4,6},{5,7},{6,4},{7,5},{8,10},{9,11},{10,... | collective-permute-start | bytes 1572872 | tf_op jit(solution)/shard_map/ppermute | solution.py:17
  180.4 101.0 %copy-start.4 = (s32[2,64]{1,0:T(2,128)S(1)}, s32[2,64]{1,0:T(2,128)}, u32[]{:S(2)}) copy-start(s32[2,64]{1,0:T(2,128)} %param.23) | copy-start | bytes 1540
Sparse Core Ops, SparseCore 0:
  51.6 62.0 reduce-scatter.1
  180.4 46.6 all-gather.1
